TPU v7x, 32 devices: a whole 2x2x4 slice. The times are simulated.
32 devices in a mesh: dp: 4 (over y, x), expert: 8 (over z, core).
Axes of the slice: x: 2, y: 2, z: 4, core: 2. Of those that a mesh axis runs over, the one named last changes fastest.
Arguments:
- saved_input: bfloat16 [1024, 2048], P(('dp', 'expert')), may hold values from -6 to 6
- output_grad: bfloat16 [1024, 2048], P(('dp', 'expert')), may hold values from -6 to 6
- route_probs: float32 [1024, 8], P(('dp', 'expert')), may hold values from 0.02 to 0.4
- expert_choice: int32 [1024, 8], P(('dp', 'expert')), may hold values from 0 to 15, all different within a row; in each aligned block of 32 rows (0 to 31, 32 to 63, ...) at most 24 rows name the same one
- slot_expert: int32 [4, 8], replicated, may hold values from 0 to 15, as said below
- frozen_gate: bfloat16 [32, 2048, 768], P(('dp', 'expert')), as said below
- frozen_up: bfloat16 [32, 2048, 768], P(('dp', 'expert')), as said below
- frozen_down: bfloat16 [32, 768, 2048], P(('dp', 'expert')), as said below
- adapter_in: float32 [16, 64, 768], P('expert', 'dp'), may hold values from -0.21875 to 0.21875
- adapter_out: float32 [16, 64, 2048], P('expert', 'dp'), may hold values from -0.125 to 0.125
- moment_in: float32 [16, 64, 768], P('expert', 'dp'), may hold values from -3 to 3
- moment_out: float32 [16, 64, 2048], P('expert', 'dp'), may hold values from -3 to 3
- second_in: float32 [16, 64, 768], P('expert', 'dp'), may hold values from 0.01 to 1
- second_out: float32 [16, 64, 2048], P('expert', 'dp'), may hold values from 0.01 to 1
Outputs:
- input_grad: bfloat16 [1024, 2048], P(('dp', 'expert'))
- step_in: float32 [16, 64, 768], P('expert', 'dp')
- step_out: float32 [16, 64, 2048], P('expert', 'dp')
- momentum_in: float32 [16, 64, 768], P('expert', 'dp')
- momentum_out: float32 [16, 64, 2048], P('expert', 'dp')
- variance_in: float32 [16, 64, 768], P('expert', 'dp')
- variance_out: float32 [16, 64, 2048], P('expert', 'dp')
- replica_in: bfloat16 [32, 64, 768], P(('dp', 'expert'))
- replica_out: bfloat16 [32, 64, 2048], P(('dp', 'expert'))
Inputs may be any that keep to these rules, and one draw needn't show every extreme that they name: `expert_choice`: among the rows of one device no expert is named more than 24 times. `slot_expert`: the slots of index j of the expert axis host only experts 2 * j to 2 * j + 1, and each of these at least once. `frozen_gate`: slots that host the same expert hold the same frozen weights. `frozen_up`: slots that host the same expert hold the same frozen weights. `frozen_down`: slots that host the same expert hold the same frozen weights.
All inputs are finite; a program needn't handle non-finite values.
Results may differ from a plain program's by a relative error of at most 0.012.
Values may be sent and summed in bfloat16 or wider, within the bound.
No kernel may reach another device: no remote copies, remote signals or barrier semaphores. Data moves between devices by JAX's collectives and lax.ppermute only.
A program may use at most 128 MiB of HBM per device.

v0:
```python
import jax
import jax.numpy as jnp
from jax import lax
from jax.sharding import PartitionSpec as P

STEP = 100
adapter_scale_factor = 2.0
beta_one = 0.9
beta_two = 0.999
decay_rate = 0.01
adam_eps = 1e-08


def contract_product(left, right, left_dim, right_dim):
    return lax.dot_general(
        left, right, (((left_dim,), (right_dim,)), ((), ())), preferred_element_type=jnp.float32
    )


def route_rows(choice_flat, slot_expert, source, local_experts):
    column = choice_flat // local_experts
    hosted = (jnp.take(slot_expert, column, axis=1) == choice_flat[None, :]).astype(jnp.int32)
    counts = jnp.sum(hosted, axis=0)
    picked = source % counts
    running = jnp.cumsum(hosted, axis=0) - 1
    chosen = hosted * (running == picked[None, :]).astype(jnp.int32)
    dp_ids = jnp.arange(hosted.shape[0], dtype=jnp.int32)
    dest_row = jnp.sum(chosen * dp_ids[:, None], axis=0)
    row_ids = jnp.arange(choice_flat.shape[0], dtype=jnp.int32)
    earlier = (choice_flat[None, :] == choice_flat[:, None]) & (row_ids[None, :] < row_ids[:, None])
    rank = jnp.sum(earlier.astype(jnp.int32), axis=1)
    return (dest_row, column, rank)


def pack_rows(saved_input, scaled, position, buffer_size, top_count, shape_out):
    row_count = scaled.shape[0]
    row_ids = jnp.arange(row_count, dtype=jnp.int32)
    filler = jnp.full((buffer_size,), row_count, jnp.int32).at[position].set(row_ids)
    send_input = jnp.take(saved_input, filler // top_count, axis=0, mode="fill", fill_value=0)
    send_grad = jnp.take(scaled, filler, axis=0, mode="fill", fill_value=0)
    return (send_input.reshape(shape_out), send_grad.reshape(shape_out))


def adamw(param, grad, first, second):
    first_new = beta_one * first + (1.0 - beta_one) * grad
    second_new = beta_two * second + (1.0 - beta_two) * grad * grad
    corr_one = 1.0 - beta_one**STEP
    corr_two = 1.0 - beta_two**STEP
    step_dir = (
        first_new / corr_one / (jnp.sqrt(second_new / corr_two) + adam_eps) + decay_rate * param
    )
    return (step_dir, first_new, second_new)


def per_device(
    saved_input,
    output_grad,
    route_probs,
    expert_choice,
    slot_expert,
    frozen_gate,
    frozen_up,
    frozen_down,
    adapter_in,
    adapter_out,
    moment_in,
    moment_out,
    second_in,
    second_out,
):
    dp_count = lax.axis_size("dp")
    expert_count = lax.axis_size("expert")
    dp_index = lax.axis_index("dp")
    column_index = lax.axis_index("expert")
    local_experts = adapter_in.shape[0]
    token_count, top_count = expert_choice.shape
    width = saved_input.shape[1]
    row_count = token_count * top_count
    capacity = max(2, -(-3 * row_count // (2 * local_experts * expert_count)))
    buffer_size = dp_count * expert_count * capacity
    source = dp_index * expert_count + column_index
    choice_flat = expert_choice.reshape(row_count)
    dest_row, column, rank = route_rows(choice_flat, slot_expert, source, local_experts)
    scaled = (
        (route_probs[:, :, None] * output_grad[:, None, :].astype(jnp.float32))
        .astype(jnp.bfloat16)
        .reshape(row_count, width)
    )
    col_size = local_experts * expert_count * capacity
    col_position = (choice_flat % local_experts * expert_count + column) * capacity + rank
    col_shape = (local_experts, expert_count, capacity, width)
    col_input, col_grad = pack_rows(
        saved_input, scaled, col_position, col_size, top_count, col_shape
    )
    got_input, got_grad = (
        lax.all_to_all(col_input, "expert", split_axis=1, concat_axis=1, tiled=True),
        lax.all_to_all(col_grad, "expert", split_axis=1, concat_axis=1, tiled=True),
    )
    column_hosts = lax.dynamic_index_in_dim(slot_expert, column_index, 1, keepdims=False)
    dp_ids = jnp.arange(dp_count, dtype=jnp.int32)
    same_host = (column_hosts[:, None] == column_hosts[None, :]).astype(jnp.int32)
    host_count = jnp.sum(same_host, axis=1)
    host_place = jnp.sum(same_host * (dp_ids[None, :] < dp_ids[:, None]).astype(jnp.int32), axis=1)
    sources = dp_index * expert_count + jnp.arange(expert_count, dtype=jnp.int32)
    serves = sources[None, :] % host_count[:, None] == host_place[:, None]
    local_of = column_hosts - local_experts * column_index
    kept_mask = serves[:, :, None, None]
    zero_value = jnp.zeros((), jnp.bfloat16)
    picked_input = jnp.where(kept_mask, jnp.take(got_input, local_of, axis=0), zero_value)
    picked_grad = jnp.where(kept_mask, jnp.take(got_grad, local_of, axis=0), zero_value)
    arrived_input, arrived_grad = (
        lax.all_to_all(picked_input, "dp", split_axis=0, concat_axis=0, tiled=True),
        lax.all_to_all(picked_grad, "dp", split_axis=0, concat_axis=0, tiled=True),
    )
    fetched_in, fetched_out = (
        lax.all_gather(adapter_in.astype(jnp.bfloat16), "dp", axis=1, tiled=True),
        lax.all_gather(adapter_out.astype(jnp.bfloat16), "dp", axis=1, tiled=True),
    )
    hosted_local = slot_expert[dp_index, column_index] - local_experts * column_index
    owned_input = lax.dynamic_index_in_dim(fetched_in, hosted_local, 0, keepdims=False)
    own_out = lax.dynamic_index_in_dim(fetched_out, hosted_local, 0, keepdims=False)
    buffer_rows = arrived_input.reshape(buffer_size, width)
    gradient_row_block = arrived_grad.reshape(buffer_size, width)
    gate_weight = frozen_gate[0]
    up_weight = frozen_up[0]
    down_weight = frozen_down[0]
    gate_pre = jnp.dot(buffer_rows, gate_weight, preferred_element_type=jnp.float32)
    up_pre = jnp.dot(buffer_rows, up_weight, preferred_element_type=jnp.float32)
    sigmoid_gate = jax.nn.sigmoid(gate_pre)
    hidden_state = (gate_pre * sigmoid_gate * up_pre).astype(jnp.bfloat16)
    low_rank_input = contract_product(hidden_state, owned_input, 1, 1).astype(jnp.bfloat16)
    low_rank_gradient = contract_product(gradient_row_block, own_out, 1, 1).astype(jnp.bfloat16)
    hidden_gradient = contract_product(gradient_row_block, down_weight, 1, 1)
    hidden_gradient = hidden_gradient + adapter_scale_factor * jnp.dot(
        low_rank_gradient, owned_input, preferred_element_type=jnp.float32
    )
    up_grad = (hidden_gradient * gate_pre * sigmoid_gate).astype(jnp.bfloat16)
    gate_grad = (
        hidden_gradient * up_pre * sigmoid_gate * (1.0 + gate_pre * (1.0 - sigmoid_gate))
    ).astype(jnp.bfloat16)
    back_rows = (
        contract_product(gate_grad, gate_weight, 1, 1) + contract_product(up_grad, up_weight, 1, 1)
    ).astype(jnp.bfloat16)
    incoming_gradient = adapter_scale_factor * contract_product(
        low_rank_gradient, hidden_state, 0, 0
    )
    outgoing_gradient = adapter_scale_factor * contract_product(
        low_rank_input, gradient_row_block, 0, 0
    )
    back_block = back_rows.reshape(dp_count, expert_count, capacity, width)
    came_back = lax.all_to_all(back_block, "dp", split_axis=0, concat_axis=0, tiled=True)
    pieces_back = []
    for which_local in range(local_experts):
        chosen_mask = (serves & (local_of == which_local)[:, None])[:, :, None, None]
        pieces_back.append(jnp.sum(jnp.where(chosen_mask, came_back, zero_value), axis=0))
    gone_back = lax.all_to_all(
        jnp.stack(pieces_back), "expert", split_axis=1, concat_axis=1, tiled=True
    )
    per_row = jnp.take(gone_back.reshape(col_size, width), col_position, axis=0)
    input_grad = jnp.sum(
        per_row.reshape(token_count, top_count, width).astype(jnp.float32), axis=1
    ).astype(jnp.bfloat16)
    selector = (jnp.arange(local_experts, dtype=jnp.int32) == hosted_local).astype(jnp.float32)
    placed_in = selector[:, None, None] * incoming_gradient[None, :, :]
    placed_out = selector[:, None, None] * outgoing_gradient[None, :, :]
    summed_in, summed_out = (
        lax.psum_scatter(placed_in, "dp", scatter_dimension=1, tiled=True),
        lax.psum_scatter(placed_out, "dp", scatter_dimension=1, tiled=True),
    )
    step_in, momentum_in, variance_in = adamw(adapter_in, summed_in, moment_in, second_in)
    step_out, momentum_out, variance_out = adamw(adapter_out, summed_out, moment_out, second_out)
    copied_in, copied_out = (
        lax.all_gather(step_in.astype(jnp.bfloat16), "dp", axis=1, tiled=True),
        lax.all_gather(step_out.astype(jnp.bfloat16), "dp", axis=1, tiled=True),
    )
    replica_in = lax.dynamic_index_in_dim(copied_in, hosted_local, 0, keepdims=True)
    replica_out = lax.dynamic_index_in_dim(copied_out, hosted_local, 0, keepdims=True)
    return (
        input_grad,
        step_in,
        step_out,
        momentum_in,
        momentum_out,
        variance_in,
        variance_out,
        replica_in,
        replica_out,
    )


def solution(mesh):
    return jax.shard_map(
        per_device,
        mesh=mesh,
        in_specs=(
            P(("dp", "expert"), None),
            P(("dp", "expert"), None),
            P(("dp", "expert"), None),
            P(("dp", "expert"), None),
            P(),
            P(("dp", "expert"), None, None),
            P(("dp", "expert"), None, None),
            P(("dp", "expert"), None, None),
            P("expert", "dp", None),
            P("expert", "dp", None),
            P("expert", "dp", None),
            P("expert", "dp", None),
            P("expert", "dp", None),
            P("expert", "dp", None),
        ),
        out_specs=(
            P(("dp", "expert"), None),
            P("expert", "dp", None),
            P("expert", "dp", None),
            P("expert", "dp", None),
            P("expert", "dp", None),
            P("expert", "dp", None),
            P("expert", "dp", None),
            P(("dp", "expert"), None, None),
            P(("dp", "expert"), None, None),
        ),
        check_vma=False,
    )
```

profile of v0, /device:TPU:0, one launch (start us, length us, event | category | flops | bytes accessed | tf_op | source)
XLA Modules:
  0.0 375.1 jit_solution(5800526938693478548)
XLA Ops:
  10.6 6.0 %gather_fusion.1 = bf16[384,2048]{1,0:T(8,128)(2,1)} fusion(bf16[32,2048]{1,0:T(8,128)(2,1)} %param.16, s32[1024]{0:T(1024)S(1)} %pad_clamp_fusion.1), kind=kCustom, calls=%fused_computation.3 | custom fusion | bytes 3147264 | tf_op jit(solution)/shard_map/jit(_take)/gather | solution.py:39
  19.4 6.5 %all-to-all-start.2 = ((bf16[2,8,24,2048]{3,2,0,1:T(8,128)(2,1)}), bf16[2,8,24,2048]{3,2,0,1:T(8,128)(2,1)}, u32[]{:S(2)}, u32[]{:S(2)}) async-start(bf16[2,8,24,2048]{3,2,0,1:T(8,128)(2,1)} %copy_select_fusion), calls=%async_computation.2 | async-start | bytes 3145728 | tf_op jit(solution)/shard_map/all_to_all | solution.py:96
  29.3 6.4 %gather_fusion = bf16[384,2048]{1,0:T(8,128)(2,1)} fusion(bf16[256,2048]{1,0:T(8,128)(2,1)} %fusion.9, s32[1024]{0:T(1024)S(1)} %pad_clamp_fusion.3), kind=kCustom, calls=%fused_computation.2 | custom fusion | bytes 3147264 | tf_op jit(solution)/shard_map/jit(_take)/gather | solution.py:40
  38.5 25.2 %all-to-all-done.2 = bf16[2,8,24,2048]{3,2,0,1:T(8,128)(2,1)} async-done(((bf16[2,8,24,2048]{3,2,0,1:T(8,128)(2,1)}), bf16[2,8,24,2048]{3,2,0,1:T(8,128)(2,1)}, u32[]{:S(2)}, u32[]{:S(2)}) %all-to-all-start.2) | async-done | bytes 1572896 | tf_op jit(solution)/shard_map/all_to_all | solution.py:96
  63.8 4.3 %all-to-all-start = ((bf16[2,8,24,2048]{3,2,0,1:T(8,128)(2,1)}), bf16[2,8,24,2048]{3,2,0,1:T(8,128)(2,1)}, u32[]{:S(2)}, u32[]{:S(2)}) async-start(bf16[2,8,24,2048]{3,2,0,1:T(8,128)(2,1)} %copy_select_fusion.1), calls=%async_computation | async-start | bytes 3145728 | tf_op jit(solution)/shard_map/all_to_all | solution.py:97
  73.7 32.2 %all-to-all-done = bf16[2,8,24,2048]{3,2,0,1:T(8,128)(2,1)} async-done(((bf16[2,8,24,2048]{3,2,0,1:T(8,128)(2,1)}), bf16[2,8,24,2048]{3,2,0,1:T(8,128)(2,1)}, u32[]{:S(2)}, u32[]{:S(2)}) %all-to-all-start) | async-done | bytes 1572896 | tf_op jit(solution)/shard_map/all_to_all | solution.py:97
  109.7 5.3 %select_select_fusion.1 = (bf16[4,8,24,2048]{3,2,1,0:T(8,128)(2,1)}, bf16[4,8,24,2048]{3,2,1,0:T(8,128)(2,1)S(1)}) fusion(bf16[4,8,24,2048]{3,2,1,0:T(8,128)(2,1)} %gather_fusion.3, pred[4]{0:T(512)(128)(4,1)S(1)} %get-tuple-element.26, pred[4,8]{1,0:T(4,128)(4,1)S(1)} %get-tuple-element.25, bf16[4,8,24,2048]{3,2,1,0:T(8,128)(2,1)} %gather_fusion.4), kind=kLoop, calls=%fused_computation.17 | loop fusion | flops 6291456 | bytes 12582948 | tf_op jit(solution)/shard_map/jit(_where)/select_n | solution.py:110
  115.0 39.9 %all_to_all.30 = bf16[4,8,24,2048]{3,2,1,0:T(8,128)(2,1)} all-to-all(bf16[4,8,24,2048]{3,2,1,0:T(8,128)(2,1)S(1)} %get-tuple-element.33), channel_id=1, replica_groups=mesh['dp'=4,'expert'=8] {'dp'}, dimensions={0} | all-to-all | bytes 6291456 | tf_op jit(solution)/shard_map/all_to_all | solution.py:112
  155.0 4.8 %all-to-all-start.1 = ((bf16[4,8,24,2048]{3,2,1,0:T(8,128)(2,1)}), bf16[4,8,24,2048]{3,2,1,0:T(8,128)(2,1)}, u32[]{:S(2)}, u32[]{:S(2)}) async-start(bf16[4,8,24,2048]{3,2,1,0:T(8,128)(2,1)} %get-tuple-element.32), calls=%async_computation.1 | async-start | bytes 6291456 | tf_op jit(solution)/shard_map/all_to_all | solution.py:113
  161.1 37.8 %all_gather.13 = bf16[2,64,768]{2,1,0:T(8,128)(2,1)S(1)} all-gather(bf16[2,16,768]{2,1,0:T(8,128)(2,1)S(1)} %convert_element_type.64), channel_id=1, replica_groups=mesh['dp'=4,'expert'=8] {'dp'}, dimensions={1}, use_global_device_ids=true | all-gather | bytes 245760 | tf_op jit(solution)/shard_map/all_gather | solution.py:116
  199.0 5.6 %fusion.2 = f32[768,768]{1,0:T(8,128)S(1)} fusion(bf16[768,2048]{1,0:T(8,128)(2,1)} %bitcast.55, bf16[1,2048,768]{2,1,0:T(8,128)(2,1)} %param.21), kind=kOutput, calls=%fused_computation.9 | convolution fusion | flops 2415919104 | bytes 8650752 | tf_op jit(solution)/shard_map/dot_general | solution.py:127
  206.0 4.5 %multiply_convert_fusion = (bf16[768,768]{1,0:T(8,128)(2,1)}, f32[768,768]{1,0:T(8,128)}) fusion(f32[768,768]{1,0:T(8,128)S(1)} %fusion.2, bf16[768,2048]{1,0:T(8,128)(2,1)S(1)} %bitcast.56, bf16[1,2048,768]{2,1,0:T(8,128)(2,1)S(1)} %copy-done), kind=kOutput, calls=%fused_computation.20 | convolution fusion | flops 2419458048 | bytes 12189696 | tf_op jit(solution)/shard_map/dot_general | solution.py:128
  210.5 4.3 %convolution_multiply_fusion = f32[64,2048]{1,0:T(8,128)} fusion(bf16[768,2048]{1,0:T(8,128)(2,1)} %bitcast.4, bf16[768,768]{1,0:T(8,128)(2,1)} %get-tuple-element.34, bf16[2,64,768]{2,1,0:T(8,128)(2,1)S(1)} %all_gather.13, s32[]{:T(128)S(6)} %select_n.159), kind=kOutput, calls=%fused_computation.25 | convolution fusion | flops 277004288 | bytes 4947972 | tf_op jit(solution)/shard_map/dot_general | solution.py:15
  217.0 6.9 %fusion.7 = f32[768,768]{1,0:T(8,128)} fusion(bf16[768,2048]{1,0:T(8,128)(2,1)} %bitcast.4, bf16[1,768,2048]{2,1,0:T(8,128)(2,1)} %param.23), kind=kOutput, calls=%fused_computation.14 | convolution fusion | flops 2415919104 | bytes 8650752 | tf_op jit(solution)/shard_map/dot_general | solution.py:15
  223.9 20.0 %reduce-scatter.5.cloned.1.call-done = f32[2,16,2048]{2,1,0:T(8,128)} async-done(((f32[2,64,2048]{2,1,0:T(8,128)}), f32[2,16,2048]{2,1,0:T(8,128)}) %reduce-scatter.5.cloned.1.call-update) | async-done | bytes 262160 | tf_op jit(solution)/shard_map/reduce_scatter | solution.py:168
  246.2 10.3 %all_gather.12 = bf16[2,64,2048]{2,1,0:T(8,128)(2,1)S(1)} all-gather(bf16[2,16,2048]{2,1,0:T(8,128)(2,1)S(1)} %get-tuple-element.30), channel_id=1, replica_groups=mesh['dp'=4,'expert'=8] {'dp'}, dimensions={1}, use_global_device_ids=true | all-gather | bytes 655360 | tf_op jit(solution)/shard_map/all_gather | solution.py:117
  265.0 4.2 %add_convert_fusion = bf16[768,2048]{1,0:T(8,128)(2,1)} fusion(f32[768,2048]{1,0:T(8,128)S(1)} %fusion, bf16[1,2048,768]{2,1,0:T(8,128)(2,1)S(1)} %copy-done, f32[768,768]{1,0:T(8,128)S(1)} %multiply_add_fusion, f32[768,768]{1,0:T(8,128)S(1)} %copy-done.21), kind=kOutput, calls=%fused_computation.6 | convolution fusion | flops 2422603776 | bytes 17301504 | tf_op jit(solution)/shard_map/dot_general | solution.py:15
  269.2 4.8 %all-to-all-start.4 = ((bf16[4,8,24,2048]{3,2,1,0:T(8,128)(2,1)}), bf16[4,8,24,2048]{3,2,1,0:T(8,128)(2,1)}, u32[]{:S(2)}, u32[]{:S(2)}) async-start(bf16[4,8,24,2048]{3,2,1,0:T(8,128)(2,1)} %bitcast.57), calls=%async_computation.4 | async-start | bytes 6291456 | tf_op jit(solution)/shard_map/all_to_all | solution.py:151
  274.1 34.1 %all-to-all-done.4 = bf16[4,8,24,2048]{3,2,1,0:T(8,128)(2,1)} async-done(((bf16[4,8,24,2048]{3,2,1,0:T(8,128)(2,1)}), bf16[4,8,24,2048]{3,2,1,0:T(8,128)(2,1)}, u32[]{:S(2)}, u32[]{:S(2)}) %all-to-all-start.4) | async-done | bytes 3145760 | tf_op jit(solution)/shard_map/all_to_all | solution.py:151
  313.3 4.8 %all-to-all-start.5 = ((bf16[2,8,24,2048]{3,2,0,1:T(8,128)(2,1)}), bf16[2,8,24,2048]{3,2,0,1:T(8,128)(2,1)}, u32[]{:S(2)}, u32[]{:S(2)}) async-start(bf16[2,8,24,2048]{3,2,0,1:T(8,128)(2,1)} %pad_maximum_fusion), calls=%async_computation.5 | async-start | bytes 3145728 | tf_op jit(solution)/shard_map/all_to_all | solution.py:156
  320.7 11.7 %all_gather.15 = bf16[2,64,2048]{2,1,0:T(8,128)(2,1)S(1)} all-gather(bf16[2,16,2048]{2,1,0:T(8,128)(2,1)S(1)} %copy-done.3), channel_id=1, replica_groups=mesh['dp'=4,'expert'=8] {'dp'}, dimensions={1}, use_global_device_ids=true | all-gather | bytes 655360 | tf_op jit(solution)/shard_map/all_gather | solution.py:174
  333.1 13.8 %reduce-scatter.3.cloned.1.call-done = f32[2,16,768]{2,1,0:T(8,128)} async-done(((f32[2,64,768]{2,1,0:T(8,128)}), f32[2,16,768]{2,1,0:T(8,128)}) %reduce-scatter.3.cloned.1.call-update) | async-done | bytes 98320 | tf_op jit(solution)/shard_map/reduce_scatter | solution.py:167
  348.6 8.9 %all_gather.14 = bf16[2,64,768]{2,1,0:T(8,128)(2,1)S(1)} all-gather(bf16[2,16,768]{2,1,0:T(8,128)(2,1)S(1)} %get-tuple-element.20), channel_id=1, replica_groups=mesh['dp'=4,'expert'=8] {'dp'}, dimensions={1}, use_global_device_ids=true | all-gather | bytes 245760 | tf_op jit(solution)/shard_map/all_gather | solution.py:173
  360.9 5.0 %gather_fusion.2 = bf16[256,2048]{1,0:T(8,128)(2,1)} fusion(bf16[384,2048]{1,0:T(8,128)(2,1)} %bitcast.52, s32[1024]{0:T(1024)S(1)} %pad_clamp_fusion), kind=kCustom, calls=%fused_computation.4 | custom fusion | bytes 2098176 | tf_op jit(solution)/shard_map/jit(_take)/gather | solution.py:159
  (105 shorter events, 53.0 us)
Async XLA Ops:
  7.2 198.8 %copy-start = (bf16[1,2048,768]{2,1,0:T(8,128)(2,1)S(1)}, bf16[1,2048,768]{2,1,0:T(8,128)(2,1)}, u32[]{:S(2)}) copy-start(bf16[1,2048,768]{2,1,0:T(8,128)(2,1)} %param.22) | copy-start | bytes 9437188
  10.5 6.1 %copy-start.6 = (s32[384]{0:T(512)}, s32[384]{0:T(512)S(1)}, u32[]{:S(2)}) copy-start(s32[384]{0:T(512)S(1)} %scatter_custom_fusion) | copy-start | bytes 4612
  19.4 7.2 %copy-start.5 = (bf16[32,2048]{1,0:T(8,128)(2,1)S(1)}, bf16[32,2048]{1,0:T(8,128)(2,1)}, u32[]{:S(2)}) copy-start(bf16[32,2048]{1,0:T(8,128)(2,1)} %param.17) | copy-start | bytes 393220
  19.4 44.4 %all-to-all-start.2 = ((bf16[2,8,24,2048]{3,2,0,1:T(8,128)(2,1)}), bf16[2,8,24,2048]{3,2,0,1:T(8,128)(2,1)}, u32[]{:S(2)}, u32[]{:S(2)}) async-start(bf16[2,8,24,2048]{3,2,0,1:T(8,128)(2,1)} %copy_select_fusion), calls=%async_computation.2 | async-start | bytes 3145728 | tf_op jit(solution)/shard_map/all_to_all | solution.py:96
  29.3 6.4 %copy-start.7 = (pred[2,8,24]{2,0,1:T(4,128)(4,1)S(1)}, pred[2,8,24]{2,0,1:T(4,128)(4,1)}, u32[]{:S(2)}) copy-start(pred[2,8,24]{2,0,1:T(4,128)(4,1)} %copy.59) | copy-start | bytes 1156
  38.5 29.5 %copy-start.8 = (s32[4,8]{1,0:T(4,128)S(1)}, s32[4,8]{1,0:T(4,128)}, u32[]{:S(2)}) copy-start(s32[4,8]{1,0:T(4,128)} %param.20) | copy-start | bytes 388
  63.8 42.1 %all-to-all-start = ((bf16[2,8,24,2048]{3,2,0,1:T(8,128)(2,1)}), bf16[2,8,24,2048]{3,2,0,1:T(8,128)(2,1)}, u32[]{:S(2)}, u32[]{:S(2)}) async-start(bf16[2,8,24,2048]{3,2,0,1:T(8,128)(2,1)} %copy_select_fusion.1), calls=%async_computation | async-start | bytes 3145728 | tf_op jit(solution)/shard_map/all_to_all | solution.py:97
  69.9 39.8 %copy-start.14 = (pred[4,8]{1,0:T(4,128)(4,1)}, pred[4,8]{1,0:T(4,128)(4,1)S(1)}, u32[]{:S(2)}) copy-start(pred[4,8]{1,0:T(4,128)(4,1)S(1)} %get-tuple-element.25) | copy-start | bytes 100
  155.0 6.1 %copy-start.4 = (f32[2,16,768]{2,1,0:T(8,128)S(1)}, f32[2,16,768]{2,1,0:T(8,128)}, u32[]{:S(2)}) copy-start(f32[2,16,768]{2,1,0:T(8,128)} %param.24) | copy-start | bytes 294916
  155.0 55.5 %all-to-all-start.1 = ((bf16[4,8,24,2048]{3,2,1,0:T(8,128)(2,1)}), bf16[4,8,24,2048]{3,2,1,0:T(8,128)(2,1)}, u32[]{:S(2)}, u32[]{:S(2)}) async-start(bf16[4,8,24,2048]{3,2,1,0:T(8,128)(2,1)} %get-tuple-element.32), calls=%async_computation.1 | async-start | bytes 6291456 | tf_op jit(solution)/shard_map/all_to_all | solution.py:113
  159.8 84.1 %reduce-scatter.5.cloned.1.call-start = ((), (), s32[]{:S(2)}) async-start(), calls=%async_computation.9 | async-start | bytes 1310720 | tf_op jit(solution)/shard_map/reduce_scatter | solution.py:168
  199.0 15.8 %copy-start.16 = (f32[2]{0:T(128)}, f32[2]{0:T(128)S(1)}, u32[]{:S(2)}) copy-start(f32[2]{0:T(128)S(1)} %compare_convert_fusion) | copy-start | bytes 28
  199.0 7.0 %copy-start.1 = (bf16[4,8,24,2048]{3,2,1,0:T(8,128)(2,1)S(1)}, bf16[4,8,24,2048]{3,2,1,0:T(8,128)(2,1)}, u32[]{:S(2)}) copy-start(bf16[4,8,24,2048]{3,2,1,0:T(8,128)(2,1)} %all_to_all.30) | copy-start | bytes 9437188
  256.5 4.0 %copy-start.22 = (f32[768,768]{1,0:T(8,128)S(1)}, f32[768,768]{1,0:T(8,128)}, u32[]{:S(2)}) copy-start(f32[768,768]{1,0:T(8,128)} %get-tuple-element.35) | copy-start | bytes 7077892
  269.2 4.8 %copy-start.15 = (pred[4,8]{1,0:T(4,128)(4,1)S(1)}, pred[4,8]{1,0:T(4,128)(4,1)}, u32[]{:S(2)}) copy-start(pred[4,8]{1,0:T(4,128)(4,1)} %copy-done.14) | copy-start | bytes 100
  269.2 4.8 %copy-start.18 = (pred[4]{0:T(512)(128)(4,1)S(1)}, pred[4]{0:T(512)(128)(4,1)}, u32[]{:S(2)}) copy-start(pred[4]{0:T(512)(128)(4,1)} %get-tuple-element.12) | copy-start | bytes 16
  269.2 39.0 %copy-start.13 = (pred[4,8]{1,0:T(4,128)(4,1)S(1)}, pred[4,8]{1,0:T(4,128)(4,1)}, u32[]{:S(2)}) copy-start(pred[4,8]{1,0:T(4,128)(4,1)} %get-tuple-element.24) | copy-start | bytes 100
  269.2 39.0 %all-to-all-start.4 = ((bf16[4,8,24,2048]{3,2,1,0:T(8,128)(2,1)}), bf16[4,8,24,2048]{3,2,1,0:T(8,128)(2,1)}, u32[]{:S(2)}, u32[]{:S(2)}) async-start(bf16[4,8,24,2048]{3,2,1,0:T(8,128)(2,1)} %bitcast.57), calls=%async_computation.4 | async-start | bytes 6291456 | tf_op jit(solution)/shard_map/all_to_all | solution.py:151
  313.2 6.4 %copy-start.17 = (f32[2]{0:T(128)S(1)}, f32[2]{0:T(128)}, u32[]{:S(2)}) copy-start(f32[2]{0:T(128)} %copy-done.16) | copy-start | bytes 28
  313.2 7.3 %copy-start.10 = (s32[256]{0:T(256)S(1)}, s32[256]{0:T(256)}, u32[]{:S(2)}) copy-start(s32[256]{0:T(256)} %copy-done.9) | copy-start | bytes 3076
  313.2 7.4 %copy-start.12 = (s32[256,1]{0,1:T(1,128)S(1)}, s32[256,1]{0,1:T(1,128)}, u32[]{:S(2)}) copy-start(s32[256,1]{0,1:T(1,128)} %copy-done.11) | copy-start | bytes 3076
  313.2 7.5 %copy-start.3 = (bf16[2,16,2048]{2,1,0:T(8,128)(2,1)S(1)}, bf16[2,16,2048]{2,1,0:T(8,128)(2,1)}, u32[]{:S(2)}) copy-start(bf16[2,16,2048]{2,1,0:T(8,128)(2,1)} %get-tuple-element.16) | copy-start | bytes 393220
  313.3 44.9 %all-to-all-start.5 = ((bf16[2,8,24,2048]{3,2,0,1:T(8,128)(2,1)}), bf16[2,8,24,2048]{3,2,0,1:T(8,128)(2,1)}, u32[]{:S(2)}, u32[]{:S(2)}) async-start(bf16[2,8,24,2048]{3,2,0,1:T(8,128)(2,1)} %pad_maximum_fusion), calls=%async_computation.5 | async-start | bytes 3145728 | tf_op jit(solution)/shard_map/all_to_all | solution.py:156
  318.0 28.8 %reduce-scatter.3.cloned.1.call-start = ((), (), s32[]{:S(2)}) async-start(), calls=%async_computation.8 | async-start | bytes 491520 | tf_op jit(solution)/shard_map/reduce_scatter | solution.py:167
  (6 other events, 11.4 us)
Sparse Core Ops, SparseCore 0:
  217.1 26.6 reduce-scatter.4
  321.6 25.1 reduce-scatter.2
where the time goes:
time: 376 us; the launch traced here: 375 us
  waiting for transfers between devices  125 us (33%)
  blocking collectives  109 us (29%)
  local copies, waits for them, and re-layouts  37.7 us (10%)
  matrix products  33.9 us (9%)
  other arithmetic  29.3 us (8%)
  starting transfers between devices  25.2 us (7%)
  between operations  15.1 us (4%)
    all_to_all x1, blocking collectives, per_device(): lax.all_to_all(picked_input, 'dp', split_axis=0, concat_axis=0, tiled=True)  39.9 us
    all_gather x1, blocking collectives, per_device(): lax.all_gather(adapter_in.astype(jnp.bfloat16), 'dp', axis=1, tiled=True)  37.8 us
    all_to_all x1, waiting for transfers between devices, per_device(): lax.all_to_all(back_block, 'dp', split_axis=0, concat_axis=0, tiled=True)  34.1 us
    all_to_all x1, waiting for transfers between devices, per_device(): lax.all_to_all(col_grad, 'expert', split_axis=1, concat_axis=1, tiled=True)  32.2 us
    all_to_all x1, waiting for transfers between devices, per_device(): lax.all_to_all(col_input, 'expert', split_axis=1, concat_axis=1, tiled=True)  25.2 us
    dot_general x6, matrix products, contract_product(): lax.dot_general(left, right, (((left_dim,), (right_dim,)), ((), ())), pre...  23.4 us
    reduce_scatter x1, waiting for transfers between devices, per_device(): lax.psum_scatter(placed_out, 'dp', scatter_dimension=1, tiled=True)  20 us
    reduce_scatter x1, waiting for transfers between devices, per_device(): lax.psum_scatter(placed_in, 'dp', scatter_dimension=1, tiled=True)  13.8 us
  transfers between devices with their start and end apart: 7, of which 5 were waited for; matrix products, arithmetic and copies ran while one was open for 11% of the time, Pallas kernels for 0%

commit v1 on v0

--- a/solution.py
+++ b/solution.py
@@ -113,7 +113,12 @@
         lax.all_to_all(picked_grad, "dp", split_axis=0, concat_axis=0, tiled=True),
     )
     fetched_in, fetched_out = (
-        lax.all_gather(adapter_in.astype(jnp.bfloat16), "dp", axis=1, tiled=True),
+        jnp.concatenate(
+            lax.all_to_all(
+                jnp.stack([adapter_in.astype(jnp.bfloat16)] * lax.axis_size("dp")), "dp", 0, 0
+            ),
+            axis=1,
+        ),
         lax.all_gather(adapter_out.astype(jnp.bfloat16), "dp", axis=1, tiled=True),
     )
     hosted_local = slot_expert[dp_index, column_index] - local_experts * column_index

time: 376 us -> 367 us (0.976)
  blocking collectives: 109 us -> 72.5 us
  waiting for transfers between devices: 125 us -> 146 us
    all_gather x1 -> x0, blocking collectives: 37.8 us -> none  [per_device(): lax.all_gather(adapter_in.astype(jnp.bfloat16), 'dp', axis=1, tiled=True)]
    all_to_all x1, waiting for transfers between devices: 0.01 us -> 21.1 us  [per_device(): lax.all_to_all(picked_grad, 'dp', split_axis=0, concat_axis=0, tiled=True)]
  transfers between devices with their start and end apart: 7 -> 8, of which waited for: 5 -> 6; matrix products, arithmetic and copies ran while one was open for 11% -> 14% of each run, Pallas kernels for 0% -> 0%
where the time goes in v1:
time: 367 us; the launch traced here: 366 us
  waiting for transfers between devices  146 us (40%)
  blocking collectives  72.5 us (20%)
  local copies, waits for them, and re-layouts  38.4 us (10%)
  matrix products  33.9 us (9%)
  other arithmetic  30.7 us (8%)
  starting transfers between devices  28.9 us (8%)
  between operations  15.1 us (4%)
    all_to_all x1, blocking collectives, per_device(): lax.all_to_all(picked_input, 'dp', split_axis=0, concat_axis=0, tiled=True)  41.6 us
    all_to_all x1, waiting for transfers between devices, per_device(): lax.all_to_all(back_block, 'dp', split_axis=0, concat_axis=0, tiled=True)  34.1 us
    all_to_all x1, waiting for transfers between devices, per_device(): lax.all_to_all(col_grad, 'expert', split_axis=1, concat_axis=1, tiled=True)  32.1 us
    all_to_all x1, waiting for transfers between devices, per_device(): lax.all_to_all(col_input, 'expert', split_axis=1, concat_axis=1, tiled=True)  25.3 us
    dot_general x6, matrix products, contract_product(): lax.dot_general(left, right, (((left_dim,), (right_dim,)), ((), ())), pre...  23.3 us
    all_to_all x1, waiting for transfers between devices, per_device(): lax.all_to_all(picked_grad, 'dp', split_axis=0, concat_axis=0, tiled=True)  21.1 us
    reduce_scatter x1, waiting for transfers between devices, per_device(): lax.psum_scatter(placed_out, 'dp', scatter_dimension=1, tiled=True)  20 us
    reduce_scatter x1, waiting for transfers between devices, per_device(): lax.psum_scatter(placed_in, 'dp', scatter_dimension=1, tiled=True)  13.7 us
  transfers between devices with their start and end apart: 8, of which 6 were waited for; matrix products, arithmetic and copies ran while one was open for 14% of the time, Pallas kernels for 0%

profile of v1, /device:TPU:0, one launch (start us, length us, event | category | flops | bytes accessed | tf_op | source)
XLA Modules:
  0.0 365.8 jit_solution(11812696293812238434)
XLA Ops:
  10.6 6.0 %gather_fusion.1 = bf16[384,2048]{1,0:T(8,128)(2,1)} fusion(bf16[32,2048]{1,0:T(8,128)(2,1)} %param.16, s32[1024]{0:T(1024)S(1)} %pad_clamp_fusion.1), kind=kCustom, calls=%fused_computation.3 | custom fusion | bytes 3147264 | tf_op jit(solution)/shard_map/jit(_take)/gather | solution.py:39
  19.4 6.5 %all-to-all-start.3 = ((bf16[2,8,24,2048]{3,2,0,1:T(8,128)(2,1)}), bf16[2,8,24,2048]{3,2,0,1:T(8,128)(2,1)}, u32[]{:S(2)}, u32[]{:S(2)}) async-start(bf16[2,8,24,2048]{3,2,0,1:T(8,128)(2,1)} %copy_select_fusion), calls=%async_computation.3 | async-start | bytes 3145728 | tf_op jit(solution)/shard_map/all_to_all | solution.py:96
  29.3 6.4 %gather_fusion = bf16[384,2048]{1,0:T(8,128)(2,1)} fusion(bf16[256,2048]{1,0:T(8,128)(2,1)} %fusion.9, s32[1024]{0:T(1024)S(1)} %pad_clamp_fusion.3), kind=kCustom, calls=%fused_computation.2 | custom fusion | bytes 3147264 | tf_op jit(solution)/shard_map/jit(_take)/gather | solution.py:40
  38.5 25.3 %all-to-all-done.3 = bf16[2,8,24,2048]{3,2,0,1:T(8,128)(2,1)} async-done(((bf16[2,8,24,2048]{3,2,0,1:T(8,128)(2,1)}), bf16[2,8,24,2048]{3,2,0,1:T(8,128)(2,1)}, u32[]{:S(2)}, u32[]{:S(2)}) %all-to-all-start.3) | async-done | bytes 1572896 | tf_op jit(solution)/shard_map/all_to_all | solution.py:96
  63.8 4.3 %all-to-all-start = ((bf16[2,8,24,2048]{3,2,0,1:T(8,128)(2,1)}), bf16[2,8,24,2048]{3,2,0,1:T(8,128)(2,1)}, u32[]{:S(2)}, u32[]{:S(2)}) async-start(bf16[2,8,24,2048]{3,2,0,1:T(8,128)(2,1)} %copy_select_fusion.1), calls=%async_computation | async-start | bytes 3145728 | tf_op jit(solution)/shard_map/all_to_all | solution.py:97
  73.7 32.1 %all-to-all-done = bf16[2,8,24,2048]{3,2,0,1:T(8,128)(2,1)} async-done(((bf16[2,8,24,2048]{3,2,0,1:T(8,128)(2,1)}), bf16[2,8,24,2048]{3,2,0,1:T(8,128)(2,1)}, u32[]{:S(2)}, u32[]{:S(2)}) %all-to-all-start) | async-done | bytes 1572896 | tf_op jit(solution)/shard_map/all_to_all | solution.py:97
  114.1 6.2 %select_select_fusion.1 = (bf16[4,8,24,2048]{3,2,1,0:T(8,128)(2,1)}, bf16[4,8,24,2048]{3,2,1,0:T(8,128)(2,1)}) fusion(bf16[4,8,24,2048]{3,2,1,0:T(8,128)(2,1)} %gather_fusion.3, pred[4]{0:T(512)(128)(4,1)S(1)} %get-tuple-element.26, pred[4,8]{1,0:T(4,128)(4,1)S(1)} %get-tuple-element.25, bf16[4,8,24,2048]{3,2,1,0:T(8,128)(2,1)} %gather_fusion.4), kind=kLoop, calls=%fused_computation.17 | loop fusion | flops 6291456 | bytes 12582948 | tf_op jit(solution)/shard_map/jit(_where)/select_n | solution.py:110
  120.3 41.6 %all_to_all.35 = bf16[4,8,24,2048]{3,2,1,0:T(8,128)(2,1)} all-to-all(bf16[4,8,24,2048]{3,2,1,0:T(8,128)(2,1)} %get-tuple-element.33), channel_id=1, replica_groups=mesh['dp'=4,'expert'=8] {'dp'}, dimensions={0} | all-to-all | bytes 6291456 | tf_op jit(solution)/shard_map/all_to_all | solution.py:112
  162.0 4.6 %all-to-all-start.1 = ((bf16[4,8,24,2048]{3,2,1,0:T(8,128)(2,1)}), bf16[4,8,24,2048]{3,2,1,0:T(8,128)(2,1)}, u32[]{:S(2)}, u32[]{:S(2)}) async-start(bf16[4,8,24,2048]{3,2,1,0:T(8,128)(2,1)} %get-tuple-element.32), calls=%async_computation.1 | async-start | bytes 6291456 | tf_op jit(solution)/shard_map/all_to_all | solution.py:113
  168.6 5.6 %fusion.2 = f32[768,768]{1,0:T(8,128)S(1)} fusion(bf16[768,2048]{1,0:T(8,128)(2,1)} %bitcast.58, bf16[1,2048,768]{2,1,0:T(8,128)(2,1)} %param.21), kind=kOutput, calls=%fused_computation.9 | convolution fusion | flops 2415919104 | bytes 8650752 | tf_op jit(solution)/shard_map/dot_general | solution.py:132
  175.7 4.5 %multiply_convert_fusion = (bf16[768,768]{1,0:T(8,128)(2,1)}, f32[768,768]{1,0:T(8,128)}) fusion(f32[768,768]{1,0:T(8,128)S(1)} %fusion.2, bf16[768,2048]{1,0:T(8,128)(2,1)S(1)} %bitcast.59, bf16[1,2048,768]{2,1,0:T(8,128)(2,1)S(1)} %copy-done), kind=kOutput, calls=%fused_computation.20 | convolution fusion | flops 2419458048 | bytes 12189696 | tf_op jit(solution)/shard_map/dot_general | solution.py:133
  180.2 21.1 %all-to-all-done.1 = bf16[4,8,24,2048]{3,2,1,0:T(8,128)(2,1)} async-done(((bf16[4,8,24,2048]{3,2,1,0:T(8,128)(2,1)}), bf16[4,8,24,2048]{3,2,1,0:T(8,128)(2,1)}, u32[]{:S(2)}, u32[]{:S(2)}) %all-to-all-start.1) | async-done | bytes 3145760 | tf_op jit(solution)/shard_map/all_to_all | solution.py:113
  201.3 4.3 %convolution_multiply_fusion = f32[64,2048]{1,0:T(8,128)} fusion(bf16[768,2048]{1,0:T(8,128)(2,1)} %bitcast.4, bf16[768,768]{1,0:T(8,128)(2,1)} %get-tuple-element.34, bf16[2,64,768]{2,1,0:T(8,128)(2,1)S(1)} %bitcast.63, s32[]{:T(128)S(6)} %select_n.159), kind=kOutput, calls=%fused_computation.25 | convolution fusion | flops 277004288 | bytes 4947972 | tf_op jit(solution)/shard_map/dot_general | solution.py:15
  207.8 6.9 %fusion.7 = f32[768,768]{1,0:T(8,128)} fusion(bf16[768,2048]{1,0:T(8,128)(2,1)} %bitcast.4, bf16[1,768,2048]{2,1,0:T(8,128)(2,1)} %param.23), kind=kOutput, calls=%fused_computation.14 | convolution fusion | flops 2415919104 | bytes 8650752 | tf_op jit(solution)/shard_map/dot_general | solution.py:15
  214.7 20.0 %reduce-scatter.5.cloned.1.call-done = f32[2,16,2048]{2,1,0:T(8,128)} async-done(((f32[2,64,2048]{2,1,0:T(8,128)}), f32[2,16,2048]{2,1,0:T(8,128)}) %reduce-scatter.5.cloned.1.call-update) | async-done | bytes 262160 | tf_op jit(solution)/shard_map/reduce_scatter | solution.py:173
  237.0 10.2 %all_gather.9 = bf16[2,64,2048]{2,1,0:T(8,128)(2,1)S(1)} all-gather(bf16[2,16,2048]{2,1,0:T(8,128)(2,1)S(1)} %get-tuple-element.30), channel_id=1, replica_groups=mesh['dp'=4,'expert'=8] {'dp'}, dimensions={1}, use_global_device_ids=true | all-gather | bytes 655360 | tf_op jit(solution)/shard_map/all_gather | solution.py:122
  255.8 4.1 %add_convert_fusion = bf16[768,2048]{1,0:T(8,128)(2,1)} fusion(f32[768,2048]{1,0:T(8,128)S(1)} %fusion, bf16[1,2048,768]{2,1,0:T(8,128)(2,1)S(1)} %copy-done, f32[768,768]{1,0:T(8,128)S(1)} %multiply_add_fusion, f32[768,768]{1,0:T(8,128)S(1)} %copy-done.22), kind=kOutput, calls=%fused_computation.6 | convolution fusion | flops 2422603776 | bytes 17301504 | tf_op jit(solution)/shard_map/dot_general | solution.py:15
  259.9 4.8 %all-to-all-start.5 = ((bf16[4,8,24,2048]{3,2,1,0:T(8,128)(2,1)}), bf16[4,8,24,2048]{3,2,1,0:T(8,128)(2,1)}, u32[]{:S(2)}, u32[]{:S(2)}) async-start(bf16[4,8,24,2048]{3,2,1,0:T(8,128)(2,1)} %bitcast.60), calls=%async_computation.5 | async-start | bytes 6291456 | tf_op jit(solution)/shard_map/all_to_all | solution.py:156
  264.8 34.1 %all-to-all-done.5 = bf16[4,8,24,2048]{3,2,1,0:T(8,128)(2,1)} async-done(((bf16[4,8,24,2048]{3,2,1,0:T(8,128)(2,1)}), bf16[4,8,24,2048]{3,2,1,0:T(8,128)(2,1)}, u32[]{:S(2)}, u32[]{:S(2)}) %all-to-all-start.5) | async-done | bytes 3145760 | tf_op jit(solution)/shard_map/all_to_all | solution.py:156
  304.0 4.7 %all-to-all-start.6 = ((bf16[2,8,24,2048]{3,2,0,1:T(8,128)(2,1)}), bf16[2,8,24,2048]{3,2,0,1:T(8,128)(2,1)}, u32[]{:S(2)}, u32[]{:S(2)}) async-start(bf16[2,8,24,2048]{3,2,0,1:T(8,128)(2,1)} %pad_maximum_fusion), calls=%async_computation.6 | async-start | bytes 3145728 | tf_op jit(solution)/shard_map/all_to_all | solution.py:161
  311.4 11.7 %all_gather.11 = bf16[2,64,2048]{2,1,0:T(8,128)(2,1)S(1)} all-gather(bf16[2,16,2048]{2,1,0:T(8,128)(2,1)S(1)} %copy-done.3), channel_id=1, replica_groups=mesh['dp'=4,'expert'=8] {'dp'}, dimensions={1}, use_global_device_ids=true | all-gather | bytes 655360 | tf_op jit(solution)/shard_map/all_gather | solution.py:179
  323.8 13.7 %reduce-scatter.3.cloned.1.call-done = f32[2,16,768]{2,1,0:T(8,128)} async-done(((f32[2,64,768]{2,1,0:T(8,128)}), f32[2,16,768]{2,1,0:T(8,128)}) %reduce-scatter.3.cloned.1.call-update) | async-done | bytes 98320 | tf_op jit(solution)/shard_map/reduce_scatter | solution.py:172
  339.3 8.9 %all_gather.10 = bf16[2,64,768]{2,1,0:T(8,128)(2,1)S(1)} all-gather(bf16[2,16,768]{2,1,0:T(8,128)(2,1)S(1)} %get-tuple-element.20), channel_id=1, replica_groups=mesh['dp'=4,'expert'=8] {'dp'}, dimensions={1}, use_global_device_ids=true | all-gather | bytes 245760 | tf_op jit(solution)/shard_map/all_gather | solution.py:178
  351.6 5.0 %gather_fusion.2 = bf16[256,2048]{1,0:T(8,128)(2,1)} fusion(bf16[384,2048]{1,0:T(8,128)(2,1)} %bitcast.55, s32[1024]{0:T(1024)S(1)} %pad_clamp_fusion), kind=kCustom, calls=%fused_computation.4 | custom fusion | bytes 2098176 | tf_op jit(solution)/shard_map/jit(_take)/gather | solution.py:164
  (110 shorter events, 58.1 us)
Async XLA Ops:
  7.2 168.5 %copy-start = (bf16[1,2048,768]{2,1,0:T(8,128)(2,1)S(1)}, bf16[1,2048,768]{2,1,0:T(8,128)(2,1)}, u32[]{:S(2)}) copy-start(bf16[1,2048,768]{2,1,0:T(8,128)(2,1)} %param.22) | copy-start | bytes 9437188
  10.5 6.1 %copy-start.7 = (s32[384]{0:T(512)}, s32[384]{0:T(512)S(1)}, u32[]{:S(2)}) copy-start(s32[384]{0:T(512)S(1)} %scatter_custom_fusion) | copy-start | bytes 4612
  19.4 7.2 %copy-start.6 = (bf16[32,2048]{1,0:T(8,128)(2,1)S(1)}, bf16[32,2048]{1,0:T(8,128)(2,1)}, u32[]{:S(2)}) copy-start(bf16[32,2048]{1,0:T(8,128)(2,1)} %param.17) | copy-start | bytes 393220
  19.4 44.4 %all-to-all-start.3 = ((bf16[2,8,24,2048]{3,2,0,1:T(8,128)(2,1)}), bf16[2,8,24,2048]{3,2,0,1:T(8,128)(2,1)}, u32[]{:S(2)}, u32[]{:S(2)}) async-start(bf16[2,8,24,2048]{3,2,0,1:T(8,128)(2,1)} %copy_select_fusion), calls=%async_computation.3 | async-start | bytes 3145728 | tf_op jit(solution)/shard_map/all_to_all | solution.py:96
  29.3 6.4 %copy-start.8 = (pred[2,8,24]{2,0,1:T(4,128)(4,1)S(1)}, pred[2,8,24]{2,0,1:T(4,128)(4,1)}, u32[]{:S(2)}) copy-start(pred[2,8,24]{2,0,1:T(4,128)(4,1)} %copy.61) | copy-start | bytes 1156
  38.5 29.6 %copy-start.4 = (f32[2,16,768]{2,1,0:T(8,128)S(1)}, f32[2,16,768]{2,1,0:T(8,128)}, u32[]{:S(2)}) copy-start(f32[2,16,768]{2,1,0:T(8,128)} %param.24) | copy-start | bytes 294916
  38.5 29.6 %copy-start.9 = (s32[4,8]{1,0:T(4,128)S(1)}, s32[4,8]{1,0:T(4,128)}, u32[]{:S(2)}) copy-start(s32[4,8]{1,0:T(4,128)} %param.20) | copy-start | bytes 388
  63.8 42.1 %all-to-all-start = ((bf16[2,8,24,2048]{3,2,0,1:T(8,128)(2,1)}), bf16[2,8,24,2048]{3,2,0,1:T(8,128)(2,1)}, u32[]{:S(2)}, u32[]{:S(2)}) async-start(bf16[2,8,24,2048]{3,2,0,1:T(8,128)(2,1)} %copy_select_fusion.1), calls=%async_computation | async-start | bytes 3145728 | tf_op jit(solution)/shard_map/all_to_all | solution.py:97
  69.9 44.2 %copy-start.15 = (pred[4,8]{1,0:T(4,128)(4,1)}, pred[4,8]{1,0:T(4,128)(4,1)S(1)}, u32[]{:S(2)}) copy-start(pred[4,8]{1,0:T(4,128)(4,1)S(1)} %get-tuple-element.25) | copy-start | bytes 100
  106.6 13.8 %all-to-all-start.2 = ((bf16[4,2,16,768]{3,2,1,0:T(8,128)(2,1)}), bf16[4,2,16,768]{3,2,1,0:T(8,128)(2,1)S(1)}, u32[]{:S(2)}, u32[]{:S(2)}) async-start(bf16[4,2,16,768]{3,2,1,0:T(8,128)(2,1)} %stack.16), calls=%async_computation.2 | async-start | bytes 393216 | tf_op jit(solution)/shard_map/all_to_all | solution.py:117
  162.0 39.3 %all-to-all-start.1 = ((bf16[4,8,24,2048]{3,2,1,0:T(8,128)(2,1)}), bf16[4,8,24,2048]{3,2,1,0:T(8,128)(2,1)}, u32[]{:S(2)}, u32[]{:S(2)}) async-start(bf16[4,8,24,2048]{3,2,1,0:T(8,128)(2,1)} %get-tuple-element.32), calls=%async_computation.1 | async-start | bytes 6291456 | tf_op jit(solution)/shard_map/all_to_all | solution.py:113
  166.6 68.1 %reduce-scatter.5.cloned.1.call-start = ((), (), s32[]{:S(2)}) async-start(), calls=%async_computation.10 | async-start | bytes 1310720 | tf_op jit(solution)/shard_map/reduce_scatter | solution.py:173
  168.6 7.1 %copy-start.1 = (bf16[4,8,24,2048]{3,2,1,0:T(8,128)(2,1)S(1)}, bf16[4,8,24,2048]{3,2,1,0:T(8,128)(2,1)}, u32[]{:S(2)}) copy-start(bf16[4,8,24,2048]{3,2,1,0:T(8,128)(2,1)} %all_to_all.35) | copy-start | bytes 9437188
  259.9 4.8 %copy-start.16 = (pred[4,8]{1,0:T(4,128)(4,1)S(1)}, pred[4,8]{1,0:T(4,128)(4,1)}, u32[]{:S(2)}) copy-start(pred[4,8]{1,0:T(4,128)(4,1)} %copy-done.15) | copy-start | bytes 100
  259.9 4.8 %copy-start.19 = (pred[4]{0:T(512)(128)(4,1)S(1)}, pred[4]{0:T(512)(128)(4,1)}, u32[]{:S(2)}) copy-start(pred[4]{0:T(512)(128)(4,1)} %get-tuple-element.12) | copy-start | bytes 16
  259.9 39.0 %copy-start.14 = (pred[4,8]{1,0:T(4,128)(4,1)S(1)}, pred[4,8]{1,0:T(4,128)(4,1)}, u32[]{:S(2)}) copy-start(pred[4,8]{1,0:T(4,128)(4,1)} %get-tuple-element.24) | copy-start | bytes 100
  259.9 39.0 %all-to-all-start.5 = ((bf16[4,8,24,2048]{3,2,1,0:T(8,128)(2,1)}), bf16[4,8,24,2048]{3,2,1,0:T(8,128)(2,1)}, u32[]{:S(2)}, u32[]{:S(2)}) async-start(bf16[4,8,24,2048]{3,2,1,0:T(8,128)(2,1)} %bitcast.60), calls=%async_computation.5 | async-start | bytes 6291456 | tf_op jit(solution)/shard_map/all_to_all | solution.py:156
  304.0 6.4 %copy-start.18 = (f32[2]{0:T(128)S(1)}, f32[2]{0:T(128)}, u32[]{:S(2)}) copy-start(f32[2]{0:T(128)} %compare_convert_fusion) | copy-start | bytes 28
  304.0 7.3 %copy-start.11 = (s32[256]{0:T(256)S(1)}, s32[256]{0:T(256)}, u32[]{:S(2)}) copy-start(s32[256]{0:T(256)} %copy-done.10) | copy-start | bytes 3076
  304.0 7.4 %copy-start.13 = (s32[256,1]{0,1:T(1,128)S(1)}, s32[256,1]{0,1:T(1,128)}, u32[]{:S(2)}) copy-start(s32[256,1]{0,1:T(1,128)} %copy-done.12) | copy-start | bytes 3076
  304.0 7.4 %copy-start.3 = (bf16[2,16,2048]{2,1,0:T(8,128)(2,1)S(1)}, bf16[2,16,2048]{2,1,0:T(8,128)(2,1)}, u32[]{:S(2)}) copy-start(bf16[2,16,2048]{2,1,0:T(8,128)(2,1)} %get-tuple-element.16) | copy-start | bytes 393220
  304.0 44.9 %all-to-all-start.6 = ((bf16[2,8,24,2048]{3,2,0,1:T(8,128)(2,1)}), bf16[2,8,24,2048]{3,2,0,1:T(8,128)(2,1)}, u32[]{:S(2)}, u32[]{:S(2)}) async-start(bf16[2,8,24,2048]{3,2,0,1:T(8,128)(2,1)} %pad_maximum_fusion), calls=%async_computation.6 | async-start | bytes 3145728 | tf_op jit(solution)/shard_map/all_to_all | solution.py:161
  308.7 28.8 %copy-start.5 = (f32[2,16,768]{2,1,0:T(8,128)S(1)}, f32[2,16,768]{2,1,0:T(8,128)}, u32[]{:S(2)}) copy-start(f32[2,16,768]{2,1,0:T(8,128)} %param.24) | copy-start | bytes 294916
  308.7 28.8 %reduce-scatter.3.cloned.1.call-start = ((), (), s32[]{:S(2)}) async-start(), calls=%async_computation.9 | async-start | bytes 491520 | tf_op jit(solution)/shard_map/reduce_scatter | solution.py:172
  (8 other events, 19.8 us)
Sparse Core Ops, SparseCore 0:
  208.0 26.7 reduce-scatter.4
  312.3 25.1 reduce-scatter.2
